TPU v7x, 32 devices: a whole 2x2x4 slice. The times are simulated.
32 devices in a mesh: chan: 8 (over y, x, core), win: 4 (over z).
Axes of the slice: x: 2, y: 2, z: 4, core: 2. Of those that a mesh axis runs over, the one named last changes fastest.
Arguments:
- records: float32 [16, 1024, 256], P('win', 'chan'), may hold values from -180 to 180
- sources: int32 [32], replicated, may hold values from 0 to 255, as said below
Outputs:
- correlations: float32 [32, 256, 256], P('win', None, 'chan')
Inputs may be any that keep to these rules, and one draw needn't show every extreme that they name: `sources`: source s is one of the channels s * 8 to (s + 1) * 8 - 1; the first source is channel 0 and the last is channel 256 - 1.
All inputs are finite; a program needn't handle non-finite values.
Results may differ from a plain program's by a relative error of at most 0.00022.
Values sent between devices are 32-bit elements; how exact they have to be, the bound alone decides.
A program may use at most 64 MiB of HBM per device.

v0:
```python
import math

import jax
import jax.numpy as jnp
from jax import lax
from jax.sharding import PartitionSpec as P

HIGHEST = lax.Precision.HIGHEST
AMPLITUDE_FLOOR = 0.25
WHITE_EPSILON = 1e-06


def fourier_table(length):
    freq_count = length // 2
    freqs = jnp.arange(freq_count, dtype=jnp.int32)[:, None]
    sample_index = jnp.arange(length, dtype=jnp.int32)[None, :]
    angles = (freqs * sample_index % length).astype(jnp.float32) * (2.0 * math.pi / length)
    return jnp.concatenate([jnp.cos(angles), -jnp.sin(angles)], axis=0)


def band_table(freq_count, reach):
    rows_index = jnp.arange(freq_count, dtype=jnp.int32)[:, None]
    cols_index = jnp.arange(freq_count, dtype=jnp.int32)[None, :]
    return (jnp.abs(rows_index - cols_index) <= reach).astype(jnp.float32)


def inverse_table(length, lag_count, first_bin, bin_count, factor):
    freqs = first_bin + jnp.arange(bin_count, dtype=jnp.int32)
    lag_index = jnp.arange(lag_count, dtype=jnp.int32) - lag_count // 2
    angles = (lag_index[:, None] * freqs[None, :] % length).astype(jnp.float32) * (
        2.0 * math.pi / length
    )
    weights = jnp.where(freqs == 0, 1.0, 2.0).astype(jnp.float32)[None, :] * factor
    return jnp.concatenate([weights * jnp.cos(angles), -weights * jnp.sin(angles)], axis=1)


def running_level(padded, time_count, window_span):
    window_total = padded.shape[0]
    chans = padded.shape[2]
    running = jnp.concatenate(
        [jnp.zeros((window_total, 1, chans), jnp.float32), jnp.cumsum(jnp.abs(padded), axis=1)],
        axis=1,
    )
    return (running[:, window_span:] - running[:, :time_count]) / window_span


def local(records, sources):
    chan_count = lax.axis_size("chan")
    local_windows, local_time, all_channels = records.shape
    length = local_time * chan_count
    freq_count = length // 2
    chan_width = all_channels // chan_count
    half_width = min(16, local_time)
    smooth_reach = length // 32
    window_span = 2 * half_width + 1
    lag_count = length // 4
    forward = fourier_table(length)
    band_matrix = band_table(freq_count, smooth_reach)
    pieces = lax.all_to_all(records, "chan", split_axis=2, concat_axis=1, tiled=True)
    padded = jnp.pad(pieces, ((0, 0), (half_width, half_width), (0, 0)))
    amplitude = running_level(padded, length, window_span)
    whiten_pieces = pieces / jnp.maximum(amplitude, AMPLITUDE_FLOOR)
    spectrum = jnp.einsum("kt,wtc->wkc", forward, whiten_pieces, precision=HIGHEST)
    real_part = spectrum[:, :freq_count]
    imag_part = spectrum[:, freq_count:]
    magnitude = jnp.sqrt(real_part * real_part + imag_part * imag_part)
    smoothed = (
        jnp.einsum("jk,wkc->wjc", band_matrix, magnitude, precision=HIGHEST)
        / (2 * smooth_reach + 1)
        + WHITE_EPSILON
    )
    whitened = jnp.stack([real_part / smoothed, imag_part / smoothed], axis=1)
    band_data = lax.all_to_all(whitened, "win", split_axis=2, concat_axis=0, tiled=True)
    total_windows = band_data.shape[0]
    band_count = band_data.shape[2]
    source_count = sources.shape[0]
    chan_index = lax.axis_index("chan")
    channel_ids = jnp.arange(chan_width, dtype=jnp.int32)
    per_device = source_count // chan_count
    owned_local = (
        lax.dynamic_slice_in_dim(sources, chan_index * per_device, per_device)
        - chan_index * chan_width
    )
    selector = (owned_local[:, None] == channel_ids[None, :]).astype(jnp.float32)
    chosen = jnp.einsum("sc,wafc->wafs", selector, band_data, precision=HIGHEST)
    spectra = lax.all_gather(chosen, "chan", axis=3, tiled=True)
    source_real = spectra[:, 0]
    source_imag = spectra[:, 1]
    white_real = band_data[:, 0]
    white_imag = band_data[:, 1]
    cross_real = jnp.einsum(
        "wfs,wfc->fsc", source_real, white_real, precision=HIGHEST
    ) + jnp.einsum("wfs,wfc->fsc", source_imag, white_imag, precision=HIGHEST)
    cross_imag = jnp.einsum(
        "wfs,wfc->fsc", source_real, white_imag, precision=HIGHEST
    ) - jnp.einsum("wfs,wfc->fsc", source_imag, white_real, precision=HIGHEST)
    stacked = jnp.stack([cross_real, cross_imag])
    factor = 1.0 / math.sqrt(total_windows * freq_count)
    band_start = lax.axis_index("win") * band_count
    band_table_part = inverse_table(length, lag_count, band_start, band_count, factor).reshape(
        lag_count, 2, band_count
    )
    return lax.psum_scatter(
        jnp.einsum("tak,aksc->stc", band_table_part, stacked, precision=HIGHEST),
        "win",
        scatter_dimension=0,
        tiled=True,
    )


def solution(mesh):
    placed = (P("win", "chan", None), P())
    return jax.shard_map(
        local, mesh=mesh, in_specs=placed, out_specs=P("win", None, "chan"), check_vma=False
    )
```

profile of v0, /device:TPU:6, one launch (start us, length us, event | category | flops | bytes accessed | tf_op | source)
XLA Modules:
  0.0 166.9 jit_solution(1420910097086612107)
XLA Ops:
  6.5 2.1 %copy.58 = f32[4,128,256]{1,0,2:T(4,128)} copy(f32[4,128,256]{2,1,0:T(8,128)} %param.2) | data formatting | bytes 1048576 | tf_op args[0]
  8.6 4.2 %all-to-all-start = ((f32[4,128,256]{1,0,2:T(4,128)}), f32[4,128,256]{1,0,2:T(4,128)S(1)}, u32[]{:S(2)}, u32[]{:S(2)}) async-start(f32[4,128,256]{1,0,2:T(4,128)} %copy.58), calls=%async_computation | async-start | bytes 1048576 | tf_op jit(solution)/shard_map/all_to_all | solution.py:59
  12.8 9.2 %sine_negate_fusion = (f32[512,1024]{1,0:T(8,128)}, f32[512,1024]{1,0:T(8,128)}) fusion(), kind=kLoop, calls=%fused_computation.15 | loop fusion | flops 7864320 | bytes 4194304 | tf_op jit(solution)/shard_map/neg | solution.py:18
  22.0 0.0 all-to-all-done
  22.1 0.2 abs_bitcast_fusion
  22.4 0.1 reshape.194
  22.5 36.3 %reduce-window.6 = f32[4,32,9,128]{3,2,1,0:T(8,128)S(1)} reduce-window(f32[4,32,9,128]{3,2,1,0:T(8,128)S(1)} %reshape.194, f32[]{:T(128)} %constant.22.clone.1), window={size=1x1x1x128 pad=0_0x0_0x0_0x127_0}, to_apply=%region_0.1 | reduce-window | flops 18726912 | bytes 1179652 | tf_op jit(solution)/shard_map/reduce-window
  58.7 0.3 slice.45
  59.1 0.4 copy.61
  59.5 0.1 copy.62
  59.6 0.3 broadcast_add_fusion
  59.9 0.1 reduce_window_sum.16
  60.0 6.6 %fusion.14 = f32[4,1024,32]{1,2,0:T(8,128)S(1)} fusion(f32[512,1024]{1,0:T(8,128)} %get-tuple-element.13, f32[512,1024]{1,0:T(8,128)} %get-tuple-element.14, f32[4,1056,32]{1,2,0:T(8,128)S(1)} %bitcast.87, f32[4,1152,32]{1,2,0:T(8,128)S(1)} %bitcast.86, f32[4,8,4,8,128]{4,3,2,1,0:T(8,128)S(1)} %bitcast.84), kind=kOutput, calls=%fused_computation.20 | convolution fusion | flops 1612185600 | bytes 6356992 | tf_op jit(solution)/shard_map/kt,wtc->wkc/dot_general | solution.py:63
  66.6 0.7 divide_bitcast_fusion.1
  67.3 1.1 copy.63
  68.4 0.0 copy-start.2
  68.4 2.1 %reshape.201 = f32[4,1,32768]{2,1,0:T(1,128)} reshape(f32[512,2,4,32]{3,2,1,0:T(4,128)S(1)} %bitcast.79) | data formatting | bytes 1048576
  70.5 4.9 %all-to-all-start.1 = ((f32[4,1,32768]{2,1,0:T(1,128)}), f32[4,1,32768]{2,1,0:T(1,128)S(1)}, u32[]{:S(2)}, u32[]{:S(2)}) async-start(f32[4,1,32768]{2,1,0:T(1,128)} %reshape.201), calls=%async_computation.1 | async-start | bytes 1048576 | tf_op jit(solution)/shard_map/all_to_all | solution.py:73
  75.4 0.0 reduce-scatter.2.cloned.1.call-start
  75.4 0.0 copy-done.2
  75.4 0.1 dynamic-slice_subtract_fusion
  75.5 1.3 cosine_multiply_fusion
  76.7 13.4 %all-to-all-done.1 = f32[4,1,32768]{2,1,0:T(1,128)S(1)} async-done(((f32[4,1,32768]{2,1,0:T(1,128)}), f32[4,1,32768]{2,1,0:T(1,128)S(1)}, u32[]{:S(2)}, u32[]{:S(2)}) %all-to-all-start.1) | async-done | bytes 524320 | tf_op jit(solution)/shard_map/all_to_all | solution.py:73
  90.1 0.5 broadcast.245
  90.6 2.1 %reduce = f32[4,32768]{1,0:T(4,128)S(1)} reduce(f32[4,1,32768]{2,1,0:T(1,128)S(1)} %all-to-all-done.1, f32[]{:T(128)} %broadcast.245), dimensions={1}, to_apply=%all_to_all.30.reduce_sub_computation | reduce | bytes 1048580 | tf_op jit(solution)/shard_map/all_to_all | solution.py:73
  92.8 1.1 reshape.202
  93.9 0.8 copy.64
  94.8 0.3 fusion.49
  95.1 8.9 %all_gather.3 = f32[16,2,128,32]{2,0,1,3:T(8,128)S(1)} all-gather(f32[16,2,128,4]{2,0,1,3:T(8,128)S(1)} %copy.65), channel_id=1, replica_groups=mesh['chan'=8,'win'=4] {'chan'}, dimensions={3}, use_global_device_ids=true | all-gather | bytes 589824 | tf_op jit(solution)/shard_map/all_gather | solution.py:86
  104.0 0.7 fusion.60
  104.7 0.5 copy.77
  105.3 0.5 copy.67
  105.8 1.5 copy.78
  107.3 1.4 copy.69
  108.6 0.0 copy-start
  108.6 3.6 %fusion.21 = f32[128,32,32]{2,1,0:T(8,128)S(1)} fusion(f32[16,128,32]{2,0,1:T(8,128)S(1)} %copy.67, f32[16,1,128,32]{3,0,2,1:T(8,128)S(1)} %copy.77), kind=kOutput, calls=%fused_computation.28 | convolution fusion | flops 25165824 | bytes 1048576 | tf_op jit(solution)/shard_map/wfs,wfc->fsc/dot_general | solution.py:91
  112.2 0.0 copy-done
  112.3 3.6 %fusion.19 = f32[128,32,32]{2,1,0:T(8,128)S(1)} fusion(f32[16,128,32]{2,0,1:T(8,128)S(1)} %copy-done, f32[16,1,128,32]{3,0,2,1:T(8,128)S(1)} %copy.77), kind=kOutput, calls=%fused_computation.26 | convolution fusion | flops 25165824 | bytes 1048576 | tf_op jit(solution)/shard_map/wfs,wfc->fsc/dot_general | solution.py:94
  115.9 3.9 %add_bitcast_fusion = f32[1,128,32,32]{3,2,1,0:T(8,128)S(1)} fusion(f32[128,32,32]{2,1,0:T(8,128)S(1)} %fusion.21, f32[16,128,32]{2,0,1:T(8,128)S(1)} %copy-done, f32[16,1,128,32]{3,0,2,1:T(8,128)S(1)} %copy.78), kind=kOutput, calls=%fused_computation.14 | convolution fusion | flops 25296896 | bytes 1572864 | tf_op jit(solution)/shard_map/wfs,wfc->fsc/dot_general | solution.py:93
  119.8 3.7 %subtract_bitcast_fusion = f32[1,128,32,32]{3,2,1,0:T(8,128)S(1)} fusion(f32[128,32,32]{2,1,0:T(8,128)S(1)} %fusion.19, f32[16,128,32]{2,0,1:T(8,128)S(1)} %copy.67, f32[16,1,128,32]{3,0,2,1:T(8,128)S(1)} %copy.78), kind=kOutput, calls=%fused_computation.13 | convolution fusion | flops 25296896 | bytes 1572864 | tf_op jit(solution)/shard_map/wfs,wfc->fsc/dot_general | solution.py:96
  123.5 0.0 copy-start.1
  123.5 0.6 pad_maximum_fusion
  124.1 0.3 copy-done.1
  124.4 9.1 %fusion.11 = f32[32,256,32]{1,2,0:T(8,128)} fusion(f32[2,128,32,32]{3,2,1,0:T(8,128)S(1)} %pad_maximum_fusion, f32[256,1,128]{2,0,1:T(8,128)S(1)} %copy-done.1, f32[256,1,128]{2,0,1:T(8,128)S(1)} %get-tuple-element.11), kind=kOutput, calls=%fused_computation.19 | convolution fusion | flops 805371904 | bytes 2359296 | tf_op jit(solution)/shard_map/tak,aksc->stc/dot_general | solution.py:104
  133.5 0.0 reduce-scatter.2.cloned.1.call-update
  133.6 26.5 %reduce-scatter.2.cloned.1.call-done = f32[8,256,32]{1,2,0:T(8,128)} async-done(((f32[32,256,32]{1,2,0:T(8,128)}), f32[8,256,32]{1,2,0:T(8,128)}) %reduce-scatter.2.cloned.1.call-update) | async-done | bytes 262160 | tf_op jit(solution)/shard_map/reduce_scatter | solution.py:103
  (11 shorter events, 0.2 us)
Async XLA Ops:
  8.6 13.4 %all-to-all-start = ((f32[4,128,256]{1,0,2:T(4,128)}), f32[4,128,256]{1,0,2:T(4,128)S(1)}, u32[]{:S(2)}, u32[]{:S(2)}) async-start(f32[4,128,256]{1,0,2:T(4,128)} %copy.58), calls=%async_computation | async-start | bytes 1048576 | tf_op jit(solution)/shard_map/all_to_all | solution.py:59
  68.4 7.0 %copy-start.2 = (s32[32]{0:T(128)S(1)}, s32[32]{0:T(128)}, u32[]{:S(2)}) copy-start(s32[32]{0:T(128)} %param.3) | copy-start | bytes 388
  70.5 19.6 %all-to-all-start.1 = ((f32[4,1,32768]{2,1,0:T(1,128)}), f32[4,1,32768]{2,1,0:T(1,128)S(1)}, u32[]{:S(2)}, u32[]{:S(2)}) async-start(f32[4,1,32768]{2,1,0:T(1,128)} %reshape.201), calls=%async_computation.1 | async-start | bytes 1048576 | tf_op jit(solution)/shard_map/all_to_all | solution.py:73
  75.4 84.7 %reduce-scatter.2.cloned.1.call-start = ((), (), s32[]{:S(2)}) async-start(), calls=%async_computation.3 | async-start | bytes 1310720 | tf_op jit(solution)/shard_map/reduce_scatter | solution.py:103
  108.6 3.6 %copy-start = (f32[16,128,32]{2,0,1:T(8,128)S(1)}, f32[16,128,32]{2,0,1:T(8,128)}, u32[]{:S(2)}) copy-start(f32[16,128,32]{2,0,1:T(8,128)} %copy.69) | copy-start | bytes 786436
  123.5 0.9 copy-start.1
Sparse Core Ops, SparseCore 0:
  133.7 26.3 reduce-scatter.1
where the time goes:
time: 169 us; the launch traced here: 167 us
  other arithmetic  50.1 us (30%)
  waiting for transfers between devices  39.9 us (24%)
  matrix products  31.5 us (19%)
  local copies, waits for them, and re-layouts  13.8 us (8%)
  between operations  13.6 us (8%)
  starting transfers between devices  9.08 us (5%)
  blocking collectives  8.91 us (5%)
    another operation x3, other arithmetic  36.6 us
    reduce_scatter x1, waiting for transfers between devices, local(): lax.psum_scatter(jnp.einsum('tak,aksc->stc', band_table_part, stacked, pr...  26.5 us
    all_to_all x1, waiting for transfers between devices, local(): lax.all_to_all(whitened, 'win', split_axis=2, concat_axis=0, tiled=True)  13.4 us
    neg x1, other arithmetic, fourier_table(): return jnp.concatenate([jnp.cos(angles), -jnp.sin(angles)], axis=0)  9.19 us
    dot_general x1, matrix products, local(): jnp.einsum('tak,aksc->stc', band_table_part, stacked, precision=HIGHEST)  9.09 us
    all_gather x1, blocking collectives, local(): spectra = lax.all_gather(chosen, 'chan', axis=3, tiled=True)  8.91 us
    unnamed x11, local copies, waits for them, and re-layouts  7.61 us
    dot_general x1, matrix products, local(): jnp.einsum('kt,wtc->wkc', forward, whiten_pieces, precision=HIGHEST)  6.56 us
  transfers between devices with their start and end apart: 3, of which 2 were waited for; matrix products, arithmetic and copies ran while one was open for 6% of the time, Pallas kernels for 0%

commit v1 on v0

--- a/solution.py
+++ b/solution.py
@@ -1,8 +1,12 @@
+import functools
 import math
 
 import jax
 import jax.numpy as jnp
+import numpy as np
 from jax import lax
+from jax.experimental import pallas as pl
+from jax.experimental.pallas import tpu as pltpu
 from jax.sharding import PartitionSpec as P
 
 HIGHEST = lax.Precision.HIGHEST
@@ -108,8 +112,364 @@
     )
 
 
+LANES = 128
+BF16 = jnp.bfloat16
+MESH = pl.DeviceIdType.MESH
+
+
+def bin_order(freq_count):
+    per = freq_count // 8
+    pairs = ((0, 4), (1, 7), (2, 6), (3, 5))
+    return np.concatenate([8 * np.arange(per) + m for pair in pairs for m in pair])
+
+
+def split_table(table):
+    high = table.astype(np.float32).astype(BF16)
+    low = (table - high.astype(np.float64)).astype(np.float32).astype(BF16)
+    return np.stack([high, low])
+
+
+def forward_blocks(length, time):
+    per = length // 16
+    rows = np.arange(time)[:, None]
+    blocks = []
+    for first, second in ((0, 4), (1, 7), (2, 6), (3, 5)):
+        angle1 = 2 * np.pi * ((8 * np.arange(per) + first)[None, :] * rows % length) / length
+        angle2 = 2 * np.pi * ((8 * np.arange(per) + second)[None, :] * rows % length) / length
+        c1, s1, c2, s2 = np.cos(angle1), np.sin(angle1), np.cos(angle2), np.sin(angle2)
+        if first == 0:
+            zero = np.zeros_like(c1)
+            top = np.concatenate([c1, zero, -s1, zero], axis=1)
+            low = np.concatenate([zero, c2, zero, -s2], axis=1)
+        else:
+            top = np.concatenate([c1, c2, -s1, -s2], axis=1)
+            low = np.concatenate([s1, -s2, c1, -c2], axis=1)
+        blocks.append(np.concatenate([top, low], axis=0))
+    return split_table(np.stack(blocks))
+
+
+def smooth_table(freq_count, reach):
+    order = bin_order(freq_count)
+    return (np.abs(order[:, None] - order[None, :]) <= reach).astype(np.float32).astype(BF16)
+
+
+def lag_table(length, lag_count, factor):
+    bins = bin_order(length // 2)[:, None]
+    lags = (np.arange(lag_count) - lag_count // 2)[None, :]
+    angle = 2 * np.pi * (bins * lags % length) / length
+    weight = np.where(bins == 0, 1.0, 2.0) * factor
+    return split_table(np.concatenate([weight * np.cos(angle), -weight * np.sin(angle)], axis=0))
+
+
+def halves(value):
+    high = value.astype(BF16)
+    return high, (value - high.astype(jnp.float32)).astype(BF16)
+
+
+def dot(a, b):
+    return jnp.dot(a, b, preferred_element_type=jnp.float32)
+
+
+def fused_kernel(
+    half_width, smooth_reach, chan_count, win_count, per_device,
+    src_ref, rec_ref, fwd_hbm, band_hbm, lag_hbm, out_ref,
+    xt, recv, nrm, yh, yl, mh, ml, wr, wi, gs, ch, cl, part, from_left, from_right,
+    fwd, band, lag,
+    tab_sem, a_send, a_recv, g_send, g_recv, r_send, left_sem, right_sem,
+):
+    me = lax.axis_index("chan")
+    row = lax.axis_index("win")
+    windows, time, _ = rec_ref.shape
+    rows = recv.shape[1]
+    width = rows // windows
+    freq = wr.shape[1]
+    tiles = freq // LANES
+
+    tables = [
+        pltpu.make_async_copy(hbm, vmem, tab_sem.at[i])
+        for i, (hbm, vmem) in enumerate(((fwd_hbm, fwd), (band_hbm, band), (lag_hbm, lag)))
+    ]
+    for copy in tables:
+        copy.start()
+    barrier = pltpu.get_barrier_semaphore()
+    for d in range(1, chan_count):
+        pl.semaphore_signal(
+            barrier, inc=1, device_id={"chan": lax.rem(me + d, chan_count)}, device_id_type=MESH
+        )
+    for d in range(1, win_count):
+        pl.semaphore_signal(
+            barrier, inc=1, device_id={"win": lax.rem(row + d, win_count)}, device_id_type=MESH
+        )
+    for w in range(windows):
+        for h in range(rec_ref.shape[2] // LANES):
+            tile = rec_ref[w, :, h * LANES : (h + 1) * LANES].T
+            for i in range(LANES // width):
+                xt[h * (LANES // width) + i, w * width : (w + 1) * width, :] = tile[
+                    i * width : (i + 1) * width
+                ]
+    pl.semaphore_wait(barrier, chan_count + win_count - 2)
+
+    exchange = []
+    for d in range(1, chan_count):
+        peer = lax.rem(me + d, chan_count)
+        copy = pltpu.make_async_remote_copy(
+            src_ref=xt.at[peer], dst_ref=recv.at[me], send_sem=a_send.at[d], recv_sem=a_recv.at[d],
+            device_id={"chan": peer}, device_id_type=MESH,
+        )
+        copy.start()
+        exchange.append(copy)
+    recv[me] = xt[me]
+    near_row = lax.broadcasted_iota(jnp.int32, (3 * time, time), 0) - time
+    near_col = lax.broadcasted_iota(jnp.int32, (3 * time, time), 1)
+    near = (jnp.abs(near_row - near_col) <= half_width).astype(jnp.float32).astype(BF16)
+    for copy in exchange:
+        copy.wait_recv()
+
+    for i in range(8):
+        lo, hi = max(i - 1, 0), min(i + 1, 7)
+        level = jnp.zeros((rows, time), jnp.float32)
+        for j in range(lo, hi + 1):
+            high, low = halves(jnp.abs(recv[j]))
+            weights = near[(j - i + 1) * time : (j - i + 2) * time]
+            level = level + (dot(high, weights) + dot(low, weights))
+        level = level * (1.0 / (2 * half_width + 1))
+        nrm[i] = recv[i] / jnp.maximum(level, AMPLITUDE_FLOOR)
+
+    root = math.sqrt(0.5)
+
+    def butterfly(block, _):
+        at = pl.ds(pl.multiple_of(block * width, width), width)
+        n = [nrm[i, at, :] for i in range(8)]
+        a = [n[i] + n[i + 4] for i in range(4)]
+        b = [n[i] - n[i + 4] for i in range(4)]
+        even, odd = a[0] + a[2], a[1] + a[3]
+        diff, total = root * (b[1] - b[3]), root * (b[1] + b[3])
+        pairs = (
+            (even + odd, even - odd),
+            (b[0] + diff, -(b[2] + total)),
+            (a[0] - a[2], a[3] - a[1]),
+            (b[0] - diff, b[2] - total),
+        )
+        for g, pair in enumerate(pairs):
+            for side, value in enumerate(pair):
+                high, low = halves(value)
+                yh[g, at, side * time : (side + 1) * time] = high
+                yl[g, at, side * time : (side + 1) * time] = low
+        return 0
+
+    lax.fori_loop(0, windows, butterfly, 0)
+    tables[0].wait()
+    for g in range(4):
+        at = slice(g * LANES, (g + 1) * LANES)
+        both = dot(yh[g], fwd[0, g]) + dot(yl[g], fwd[0, g]) + dot(yh[g], fwd[1, g])
+        real, imag = both[:, :LANES], both[:, LANES:]
+        wr[:, at] = real
+        wi[:, at] = imag
+        high, low = halves(jnp.sqrt(real * real + imag * imag))
+        mh[:, at] = high
+        ml[:, at] = low
+    tables[1].wait()
+    for g in range(freq // 256):
+        at = slice(g * 256, (g + 1) * 256)
+        smoothed = (dot(mh[...], band[:, at]) + dot(ml[...], band[:, at])) / (
+            2 * smooth_reach + 1
+        ) + WHITE_EPSILON
+        wr[:, at] = wr[:, at] / smoothed
+        wi[:, at] = wi[:, at] / smoothed
+
+    for i in range(per_device):
+        owned = lax.rem(src_ref[me * per_device + i], width)
+        for w in range(windows):
+            at = 2 * (windows * i + w)
+            gs[me, at : at + 1, :] = wr[pl.ds(w * width + owned, 1), :]
+            gs[me, at + 1 : at + 2, :] = wi[pl.ds(w * width + owned, 1), :]
+    gather = []
+    for d in range(1, chan_count):
+        copy = pltpu.make_async_remote_copy(
+            src_ref=gs.at[me], dst_ref=gs.at[me], send_sem=g_send.at[d], recv_sem=g_recv.at[d],
+            device_id={"chan": lax.rem(me + d, chan_count)}, device_id_type=MESH,
+        )
+        copy.start()
+        gather.append(copy)
+    for copy in gather:
+        copy.wait_recv()
+    tables[2].wait()
+
+    per_owner = chan_count // win_count
+    upper = row // 2
+    inner = lax.rem(row + upper, 2)
+
+    def owner_of(p):
+        lower = 3 - p + inner * (p // 2) * (2 * lax.rem(p, 2) - 1)
+        return lower + upper * (3 - 2 * lower)
+
+    def compute(owner):
+        for t in range(tiles):
+            at = slice(t * LANES, (t + 1) * LANES)
+            white = [
+                (wr[w * width : (w + 1) * width, at], wi[w * width : (w + 1) * width, at])
+                for w in range(windows)
+            ]
+            for u in range(per_owner):
+                for i in range(per_device):
+                    real = imag = None
+                    for w in range(windows):
+                        line = 2 * (windows * i + w)
+                        sr = gs[owner * per_owner + u, line : line + 1, at]
+                        si = gs[owner * per_owner + u, line + 1 : line + 2, at]
+                        r = sr * white[w][0] + si * white[w][1]
+                        m = sr * white[w][1] - si * white[w][0]
+                        real = r if real is None else real + r
+                        imag = m if imag is None else imag + m
+                    first = (u * per_device + i) * width
+                    for side, value in enumerate((real, imag)):
+                        high, low = halves(value)
+                        col = side * freq + t * LANES
+                        ch[first : first + width, col : col + LANES] = high
+                        cl[first : first + width, col : col + LANES] = low
+        part[owner] = dot(ch[...], lag[0]) + dot(cl[...], lag[0]) + dot(ch[...], lag[1])
+
+    def hop(owner, source, landing, sem, target):
+        return pltpu.make_async_remote_copy(
+            src_ref=source, dst_ref=landing.at[owner], send_sem=r_send.at[owner],
+            recv_sem=sem.at[owner], device_id={"win": target}, device_id_type=MESH,
+        )
+
+    def finish(owner):
+        @pl.when(owner > row)
+        def _():
+            right = hop(owner, part.at[owner], from_left, left_sem, row + 1)
+
+            @pl.when(row > 0)
+            def _():
+                right.wait_recv()
+                part[owner] = part[owner] + from_left[owner]
+
+            right.start()
+
+        @pl.when(owner < row)
+        def _():
+            left = hop(owner, part.at[owner], from_right, right_sem, row - 1)
+
+            @pl.when(row < win_count - 1)
+            def _():
+                left.wait_recv()
+                part[owner] = part[owner] + from_right[owner]
+
+            left.start()
+
+    def step(p, _):
+        compute(owner_of(p))
+
+        @pl.when(inner == 0)
+        def _():
+            finish(owner_of(p))
+
+        @pl.when((inner == 1) & (p > 0))
+        def _():
+            finish(owner_of(p - 1))
+
+        return 0
+
+    lax.fori_loop(0, win_count, step, 0)
+    out_ref[...] = part[row]
+
+    @pl.when(row > 0)
+    def _():
+        hop(row, part.at[row], from_left, left_sem, row - 1).wait_recv()
+        out_ref[...] += from_left[row]
+
+    @pl.when(row < win_count - 1)
+    def _():
+        hop(row, part.at[row], from_right, right_sem, row + 1).wait_recv()
+        out_ref[...] += from_right[row]
+
+    for copy in exchange + gather:
+        copy.wait_send()
+    for owner in range(win_count):
+        @pl.when(row != owner)
+        def _():
+            hop(owner, part.at[owner], from_left, left_sem, lax.rem(row + 1, win_count)).wait_send()
+
+
+def fused(records, sources):
+    chan_count, win_count = lax.axis_size("chan"), lax.axis_size("win")
+    windows, time, channels = records.shape
+    length = time * chan_count
+    freq = length // 2
+    width = channels // chan_count
+    rows = windows * width
+    source_count = sources.shape[0]
+    lag_count = length // 4
+    reach = length // 32
+    half_width = min(16, time)
+    owned = source_count // win_count
+    factor = 1.0 / math.sqrt(windows * win_count * freq)
+    fwd = forward_blocks(length, time)
+    band = smooth_table(freq, reach)
+    lag = lag_table(length, lag_count, factor)
+    f32 = jnp.float32
+    block = owned * width
+    per_device = source_count // chan_count
+    vmem = pl.BlockSpec(memory_space=pltpu.VMEM)
+    hbm = pl.BlockSpec(memory_space=pltpu.HBM)
+    out = pl.pallas_call(
+        functools.partial(fused_kernel, half_width, reach, chan_count, win_count, per_device),
+        out_shape=jax.ShapeDtypeStruct((block, lag_count), f32),
+        in_specs=[pl.BlockSpec(memory_space=pltpu.SMEM), vmem, hbm, hbm, hbm],
+        out_specs=vmem,
+        scratch_shapes=[
+            pltpu.VMEM((chan_count, rows, time), f32),
+            pltpu.VMEM((chan_count, rows, time), f32),
+            pltpu.VMEM((chan_count, rows, time), f32),
+            pltpu.VMEM((4, rows, 2 * time), BF16),
+            pltpu.VMEM((4, rows, 2 * time), BF16),
+            pltpu.VMEM((rows, freq), BF16),
+            pltpu.VMEM((rows, freq), BF16),
+            pltpu.VMEM((rows, freq), f32),
+            pltpu.VMEM((rows, freq), f32),
+            pltpu.VMEM((chan_count, 2 * windows * per_device, freq), f32),
+            pltpu.VMEM((block, 2 * freq), BF16),
+            pltpu.VMEM((block, 2 * freq), BF16),
+            pltpu.VMEM((win_count, block, lag_count), f32),
+            pltpu.VMEM((win_count, block, lag_count), f32),
+            pltpu.VMEM((win_count, block, lag_count), f32),
+            pltpu.VMEM(fwd.shape, BF16),
+            pltpu.VMEM(band.shape, BF16),
+            pltpu.VMEM(lag.shape, BF16),
+            pltpu.SemaphoreType.DMA((3,)),
+            pltpu.SemaphoreType.DMA((chan_count,)),
+            pltpu.SemaphoreType.DMA((chan_count,)),
+            pltpu.SemaphoreType.DMA((chan_count,)),
+            pltpu.SemaphoreType.DMA((chan_count,)),
+            pltpu.SemaphoreType.DMA((win_count,)),
+            pltpu.SemaphoreType.DMA((win_count,)),
+            pltpu.SemaphoreType.DMA((win_count,)),
+        ],
+        compiler_params=pltpu.CompilerParams(
+            collective_id=0, has_side_effects=True, vmem_limit_bytes=48 * 1024 * 1024
+        ),
+        name="interferometry",
+    )(sources, records, jnp.asarray(fwd), jnp.asarray(band), jnp.asarray(lag))
+    return out.reshape(owned, width, lag_count).transpose(0, 2, 1)
+
+
+def fits(records, sources):
+    chan_count, win_count = lax.axis_size("chan"), lax.axis_size("win")
+    time, channels = records.shape[1:]
+    width = channels // chan_count
+    return (
+        time == LANES and chan_count == 8 and win_count == 4 and channels % LANES == 0
+        and LANES % width == 0 and width % 16 == 0 and sources.shape[0] % chan_count == 0
+    )
+
+
+def body(records, sources):
+    return fused(records, sources) if fits(records, sources) else local(records, sources)
+
+
 def solution(mesh):
     placed = (P("win", "chan", None), P())
     return jax.shard_map(
-        local, mesh=mesh, in_specs=placed, out_specs=P("win", None, "chan"), check_vma=False
-    )
+        body, mesh=mesh, in_specs=placed, out_specs=P("win", None, "chan"), check_vma=False
+    )

time: 169 us -> 52.9 us (0.31)
  the two profiles are of different devices: /device:TPU:6 before, /device:TPU:0 now
where the time goes in v1:
time: 52.9 us; the launch traced here: 52.6 us
  Pallas kernels  46.7 us (88%)
  local copies, waits for them, and re-layouts  5.89 us (11%)
    pallas_call x1, Pallas kernels, fused(): pl.pallas_call(functools.partial(fused_kernel, half_width, reach, chan_co...  46.7 us
    unnamed x11, local copies, waits for them, and re-layouts  5.89 us

profile of v1, /device:TPU:0, one launch (start us, length us, event | category | flops | bytes accessed | tf_op | source)
XLA Modules:
  0.0 52.6 jit_solution(17593318870081315927)
XLA Ops:
  0.0 0.0 copy-start
  0.0 1.2 %copy-done = bf16[2,1024,256]{2,1,0:T(8,128)(2,1)S(1)} copy-done((bf16[2,1024,256]{2,1,0:T(8,128)(2,1)S(1)}, bf16[2,1024,256]{2,1,0:T(8,128)(2,1)}, u32[]{:S(2)}) %copy-start) | copy-done | bytes 1048600
  1.2 0.0 copy-start.1
  1.2 1.2 %copy-done.1 = bf16[2,4,256,256]{3,2,1,0:T(8,128)(2,1)S(1)} copy-done((bf16[2,4,256,256]{3,2,1,0:T(8,128)(2,1)S(1)}, bf16[2,4,256,256]{3,2,1,0:T(8,128)(2,1)}, u32[]{:S(2)}) %copy-start.1) | copy-done | bytes 1048600
  2.5 0.0 copy-start.2
  2.5 1.0 %copy-done.2 = f32[4,128,256]{2,1,0:T(8,128)S(1)} copy-done((f32[4,128,256]{2,1,0:T(8,128)S(1)}, f32[4,128,256]{2,1,0:T(8,128)}, u32[]{:S(2)}) %copy-start.2) | copy-done | bytes 524312
  3.5 0.0 copy-start.3
  3.5 1.0 %copy-done.3 = bf16[512,512]{1,0:T(8,128)(2,1)S(1)} copy-done((bf16[512,512]{1,0:T(8,128)(2,1)S(1)}, bf16[512,512]{1,0:T(8,128)(2,1)}, u32[]{:S(2)}) %copy-start.3) | copy-done | bytes 524312
  4.5 0.0 copy-start.4
  4.5 0.7 %copy-done.4 = s32[32]{0:T(128)S(1)} copy-done((s32[32]{0:T(128)S(1)}, s32[32]{0:T(128)}, u32[]{:S(2)}) %copy-start.4) | copy-done | bytes 152
  5.2 46.7 %interferometry.1 = f32[256,256]{1,0:T(8,128)S(1)} custom-call(s32[32]{0:T(128)S(1)} %copy-done.4, f32[4,128,256]{2,1,0:T(8,128)S(1)} %copy-done.2, bf16[2,4,256,256]{3,2,1,0:T(8,128)(2,1)S(1)} %copy-done.1, bf16[512,512]{1,0:T(8,128)(2,1)S(1)} %copy-done.3, bf16[2,1024,256]{2,1,0:T(8,128)(2,1)S(1)} %copy-done), custom_call_target="tpu_custom_call" | custom-call | tf_op jit(solution)/shard_map/interferometry/pallas_call | solution.py:416
  51.9 0.7 %copy.7 = f32[8,256,32]{1,2,0:T(8,128)} copy(f32[8,256,32]{1,2,0:T(8,128)S(1)} %bitcast.3) | data formatting | bytes 524288
Async XLA Ops:
  0.0 1.2 %copy-start = (bf16[2,1024,256]{2,1,0:T(8,128)(2,1)S(1)}, bf16[2,1024,256]{2,1,0:T(8,128)(2,1)}, u32[]{:S(2)}) copy-start(bf16[2,1024,256]{2,1,0:T(8,128)(2,1)} %constant.8.clone.lag_hbm) | copy-start | bytes 3145732
  1.2 1.2 %copy-start.1 = (bf16[2,4,256,256]{3,2,1,0:T(8,128)(2,1)S(1)}, bf16[2,4,256,256]{3,2,1,0:T(8,128)(2,1)}, u32[]{:S(2)}) copy-start(bf16[2,4,256,256]{3,2,1,0:T(8,128)(2,1)} %constant.6.clone.fwd_hbm) | copy-start | bytes 3145732
  2.5 1.0 %copy-start.2 = (f32[4,128,256]{2,1,0:T(8,128)S(1)}, f32[4,128,256]{2,1,0:T(8,128)}, u32[]{:S(2)}) copy-start(f32[4,128,256]{2,1,0:T(8,128)} %rec_ref.1) | copy-start | bytes 1572868
  3.5 1.0 %copy-start.3 = (bf16[512,512]{1,0:T(8,128)(2,1)S(1)}, bf16[512,512]{1,0:T(8,128)(2,1)}, u32[]{:S(2)}) copy-start(bf16[512,512]{1,0:T(8,128)(2,1)} %constant.7.clone.band_hbm) | copy-start | bytes 1572868
  4.5 0.7 %copy-start.4 = (s32[32]{0:T(128)S(1)}, s32[32]{0:T(128)}, u32[]{:S(2)}) copy-start(s32[32]{0:T(128)} %src_ref.1) | copy-start | bytes 388

commit v2 on v1

--- a/solution.py
+++ b/solution.py
@@ -172,46 +172,67 @@
 
 def fused_kernel(
     half_width, smooth_reach, chan_count, win_count, per_device,
-    src_ref, rec_ref, fwd_hbm, band_hbm, lag_hbm, out_ref,
-    xt, recv, nrm, yh, yl, mh, ml, wr, wi, gs, ch, cl, part, from_left, from_right,
+    src_ref, rec_hbm, fwd_hbm, band_hbm, lag_hbm, out_ref,
+    rec, xt, recv, nrm, yh, yl, mh, ml, wr, wi, gs, ch, cl, part, from_left, from_right,
     fwd, band, lag,
-    tab_sem, a_send, a_recv, g_send, g_recv, r_send, left_sem, right_sem,
+    rec_sem, tab_sem, a_send, a_recv, g_send, g_recv, r_send, left_sem, right_sem,
 ):
     me = lax.axis_index("chan")
     row = lax.axis_index("win")
-    windows, time, _ = rec_ref.shape
+    windows, time, _ = rec.shape
     rows = recv.shape[1]
     width = rows // windows
     freq = wr.shape[1]
     tiles = freq // LANES
-
+    core, x, y = lax.rem(me, 2), lax.rem(me // 2, 2), me // 4
+    upper = row // 2
+    inner = lax.rem(row + upper, 2)
+
+    def flipped(d):
+        bits = ((core, 1), (x, 2), (y, 4))
+        return me + sum(b * (1 - 2 * bit) for bit, b in bits if d & b)
+
+    barrier = pltpu.get_barrier_semaphore()
+    for d in range(1, chan_count):
+        pl.semaphore_signal(barrier, inc=1, device_id={"chan": flipped(d)}, device_id_type=MESH)
+
+    @pl.when(row > 0)
+    def _():
+        pl.semaphore_signal(barrier, inc=1, device_id={"win": row - 1}, device_id_type=MESH)
+
+    @pl.when(row < win_count - 1)
+    def _():
+        pl.semaphore_signal(barrier, inc=1, device_id={"win": row + 1}, device_id_type=MESH)
+
+    loads = [
+        pltpu.make_async_copy(rec_hbm.at[w], rec.at[w], rec_sem.at[w]) for w in range(windows)
+    ]
     tables = [
         pltpu.make_async_copy(hbm, vmem, tab_sem.at[i])
         for i, (hbm, vmem) in enumerate(((fwd_hbm, fwd), (band_hbm, band), (lag_hbm, lag)))
     ]
-    for copy in tables:
+    for copy in loads + tables:
         copy.start()
-    barrier = pltpu.get_barrier_semaphore()
-    for d in range(1, chan_count):
-        pl.semaphore_signal(
-            barrier, inc=1, device_id={"chan": lax.rem(me + d, chan_count)}, device_id_type=MESH
-        )
-    for d in range(1, win_count):
-        pl.semaphore_signal(
-            barrier, inc=1, device_id={"win": lax.rem(row + d, win_count)}, device_id_type=MESH
-        )
     for w in range(windows):
-        for h in range(rec_ref.shape[2] // LANES):
-            tile = rec_ref[w, :, h * LANES : (h + 1) * LANES].T
+        loads[w].wait()
+        for h in range(rec.shape[2] // LANES):
+            tile = rec[w, :, h * LANES : (h + 1) * LANES].T
             for i in range(LANES // width):
                 xt[h * (LANES // width) + i, w * width : (w + 1) * width, :] = tile[
                     i * width : (i + 1) * width
                 ]
-    pl.semaphore_wait(barrier, chan_count + win_count - 2)
+
+    @pl.when(inner == 0)
+    def _():
+        pl.semaphore_wait(barrier, chan_count)
+
+    @pl.when(inner == 1)
+    def _():
+        pl.semaphore_wait(barrier, chan_count + 1)
 
     exchange = []
-    for d in range(1, chan_count):
-        peer = lax.rem(me + d, chan_count)
+    for d in (6, 7, 4, 5, 2, 3, 1):
+        peer = flipped(d)
         copy = pltpu.make_async_remote_copy(
             src_ref=xt.at[peer], dst_ref=recv.at[me], send_sem=a_send.at[d], recv_sem=a_recv.at[d],
             device_id={"chan": peer}, device_id_type=MESH,
@@ -283,113 +304,148 @@
             at = 2 * (windows * i + w)
             gs[me, at : at + 1, :] = wr[pl.ds(w * width + owned, 1), :]
             gs[me, at + 1 : at + 2, :] = wi[pl.ds(w * width + owned, 1), :]
-    gather = []
-    for d in range(1, chan_count):
-        copy = pltpu.make_async_remote_copy(
+    gather = {}
+    for d in (4, 5, 1, 6, 7, 2, 3):
+        gather[d] = pltpu.make_async_remote_copy(
             src_ref=gs.at[me], dst_ref=gs.at[me], send_sem=g_send.at[d], recv_sem=g_recv.at[d],
-            device_id={"chan": lax.rem(me + d, chan_count)}, device_id_type=MESH,
+            device_id={"chan": flipped(d)}, device_id_type=MESH,
         )
-        copy.start()
-        gather.append(copy)
-    for copy in gather:
-        copy.wait_recv()
+        gather[d].start()
     tables[2].wait()
 
-    per_owner = chan_count // win_count
-    upper = row // 2
-    inner = lax.rem(row + upper, 2)
-
-    def owner_of(p):
-        lower = 3 - p + inner * (p // 2) * (2 * lax.rem(p, 2) - 1)
-        return lower + upper * (3 - 2 * lower)
-
-    def compute(owner):
+    away = (1 - upper) * (1 - y) + upper * y
+
+    def chunk_of(q):
+        p, k = q // 2, lax.rem(q, 2)
+        dx, late = lax.rem(p, 2), p // 2
+        dy = away + late * (1 - 2 * away)
+        owner = 2 * (y + dy * (1 - 2 * y)) + x + dx * (1 - 2 * x)
+        return owner, core + k * (1 - 2 * core), 4 * dy + 2 * dx + k
+
+    def compute(owner, half):
+        device = owner * 2 + half
         for t in range(tiles):
             at = slice(t * LANES, (t + 1) * LANES)
             white = [
                 (wr[w * width : (w + 1) * width, at], wi[w * width : (w + 1) * width, at])
                 for w in range(windows)
             ]
-            for u in range(per_owner):
-                for i in range(per_device):
-                    real = imag = None
-                    for w in range(windows):
-                        line = 2 * (windows * i + w)
-                        sr = gs[owner * per_owner + u, line : line + 1, at]
-                        si = gs[owner * per_owner + u, line + 1 : line + 2, at]
-                        r = sr * white[w][0] + si * white[w][1]
-                        m = sr * white[w][1] - si * white[w][0]
-                        real = r if real is None else real + r
-                        imag = m if imag is None else imag + m
-                    first = (u * per_device + i) * width
-                    for side, value in enumerate((real, imag)):
-                        high, low = halves(value)
-                        col = side * freq + t * LANES
-                        ch[first : first + width, col : col + LANES] = high
-                        cl[first : first + width, col : col + LANES] = low
-        part[owner] = dot(ch[...], lag[0]) + dot(cl[...], lag[0]) + dot(ch[...], lag[1])
-
-    def hop(owner, source, landing, sem, target):
+            for i in range(per_device):
+                real = imag = None
+                for w in range(windows):
+                    line = 2 * (windows * i + w)
+                    sr = gs[device, line : line + 1, at]
+                    si = gs[device, line + 1 : line + 2, at]
+                    r = sr * white[w][0] + si * white[w][1]
+                    m = sr * white[w][1] - si * white[w][0]
+                    real = r if real is None else real + r
+                    imag = m if imag is None else imag + m
+                for side, value in enumerate((real, imag)):
+                    high, low = halves(value)
+                    col = side * freq + t * LANES
+                    ch[i * width : (i + 1) * width, col : col + LANES] = high
+                    cl[i * width : (i + 1) * width, col : col + LANES] = low
+        part[device] = dot(ch[...], lag[0]) + dot(cl[...], lag[0]) + dot(ch[...], lag[1])
+
+    def hop(slot, landing, sem, target):
         return pltpu.make_async_remote_copy(
-            src_ref=source, dst_ref=landing.at[owner], send_sem=r_send.at[owner],
-            recv_sem=sem.at[owner], device_id={"win": target}, device_id_type=MESH,
+            src_ref=part.at[slot], dst_ref=landing.at[slot], send_sem=r_send.at[slot],
+            recv_sem=sem.at[slot], device_id={"win": target}, device_id_type=MESH,
         )
 
-    def finish(owner):
+    def finish(owner, half):
+        slot = owner * 2 + half
+
         @pl.when(owner > row)
         def _():
-            right = hop(owner, part.at[owner], from_left, left_sem, row + 1)
+            right = hop(slot, from_left, left_sem, row + 1)
 
             @pl.when(row > 0)
             def _():
                 right.wait_recv()
-                part[owner] = part[owner] + from_left[owner]
+                part[slot] = part[slot] + from_left[slot]
 
             right.start()
 
         @pl.when(owner < row)
         def _():
-            left = hop(owner, part.at[owner], from_right, right_sem, row - 1)
+            left = hop(slot, from_right, right_sem, row - 1)
 
             @pl.when(row < win_count - 1)
             def _():
                 left.wait_recv()
-                part[owner] = part[owner] + from_right[owner]
+                part[slot] = part[slot] + from_right[slot]
 
             left.start()
 
-    def step(p, _):
-        compute(owner_of(p))
+    def step(q, _):
+        owner, half, d = chunk_of(q)
+
+        @pl.when(d > 0)
+        def _():
+            pltpu.make_async_remote_copy(
+                src_ref=gs.at[me], dst_ref=gs.at[me], send_sem=g_send.at[d], recv_sem=g_recv.at[d],
+                device_id={"chan": lax.rem(me + 1, chan_count)}, device_id_type=MESH,
+            ).wait_recv()
+
+        compute(owner, half)
 
         @pl.when(inner == 0)
         def _():
-            finish(owner_of(p))
-
-        @pl.when((inner == 1) & (p > 0))
-        def _():
-            finish(owner_of(p - 1))
+            finish(owner, half)
+
+        @pl.when((inner == 1) & (q >= 4) & (q < 6))
+        def _():
+            first, side, _ = chunk_of(q - 4)
+            finish(first, side)
 
         return 0
 
-    lax.fori_loop(0, win_count, step, 0)
-    out_ref[...] = part[row]
-
-    @pl.when(row > 0)
+    chunks = 2 * win_count
+    lax.fori_loop(0, chunks, step, 0)
+
+    back = 3 * upper
+
+    def finish_back(when):
+        @pl.when((inner == 1) & (when == 0))
+        def _():
+            for k in range(2):
+                finish(back, core + k * (1 - 2 * core))
+
+    parity = x + upper * (1 - 2 * x)
+    finish_back(parity)
+
+    @pl.when(inner == 1)
     def _():
-        hop(row, part.at[row], from_left, left_sem, row - 1).wait_recv()
-        out_ref[...] += from_left[row]
-
-    @pl.when(row < win_count - 1)
-    def _():
-        hop(row, part.at[row], from_right, right_sem, row + 1).wait_recv()
-        out_ref[...] += from_right[row]
-
-    for copy in exchange + gather:
+        for q in (2, 3):
+            owner, half, _ = chunk_of(q)
+            finish(owner, half)
+
+    finish_back(1 - parity)
+
+    block = part.shape[1]
+    for k in range(2):
+        half = core + k * (1 - 2 * core)
+        slot = row * 2 + half
+        at = pl.ds(pl.multiple_of(half * block, block), block)
+        out_ref[at, :] = part[slot]
+
+        @pl.when(row < win_count - 1)
+        def _():
+            hop(slot, from_right, right_sem, row + 1).wait_recv()
+            out_ref[at, :] += from_right[slot]
+
+        @pl.when(row > 0)
+        def _():
+            hop(slot, from_left, left_sem, row - 1).wait_recv()
+            out_ref[at, :] += from_left[slot]
+
+    for copy in exchange + list(gather.values()):
         copy.wait_send()
-    for owner in range(win_count):
-        @pl.when(row != owner)
-        def _():
-            hop(owner, part.at[owner], from_left, left_sem, lax.rem(row + 1, win_count)).wait_send()
+    for slot in range(chunks):
+        @pl.when(row != slot // 2)
+        def _():
+            hop(slot, from_left, left_sem, lax.rem(row + 1, win_count)).wait_send()
 
 
 def fused(records, sources):
@@ -410,15 +466,17 @@
     lag = lag_table(length, lag_count, factor)
     f32 = jnp.float32
     block = owned * width
+    half = block // 2
     per_device = source_count // chan_count
     vmem = pl.BlockSpec(memory_space=pltpu.VMEM)
     hbm = pl.BlockSpec(memory_space=pltpu.HBM)
     out = pl.pallas_call(
         functools.partial(fused_kernel, half_width, reach, chan_count, win_count, per_device),
         out_shape=jax.ShapeDtypeStruct((block, lag_count), f32),
-        in_specs=[pl.BlockSpec(memory_space=pltpu.SMEM), vmem, hbm, hbm, hbm],
+        in_specs=[pl.BlockSpec(memory_space=pltpu.SMEM), hbm, hbm, hbm, hbm],
         out_specs=vmem,
         scratch_shapes=[
+            pltpu.VMEM(records.shape, f32),
             pltpu.VMEM((chan_count, rows, time), f32),
             pltpu.VMEM((chan_count, rows, time), f32),
             pltpu.VMEM((chan_count, rows, time), f32),
@@ -429,25 +487,26 @@
             pltpu.VMEM((rows, freq), f32),
             pltpu.VMEM((rows, freq), f32),
             pltpu.VMEM((chan_count, 2 * windows * per_device, freq), f32),
-            pltpu.VMEM((block, 2 * freq), BF16),
-            pltpu.VMEM((block, 2 * freq), BF16),
-            pltpu.VMEM((win_count, block, lag_count), f32),
-            pltpu.VMEM((win_count, block, lag_count), f32),
-            pltpu.VMEM((win_count, block, lag_count), f32),
+            pltpu.VMEM((half, 2 * freq), BF16),
+            pltpu.VMEM((half, 2 * freq), BF16),
+            pltpu.VMEM((2 * win_count, half, lag_count), f32),
+            pltpu.VMEM((2 * win_count, half, lag_count), f32),
+            pltpu.VMEM((2 * win_count, half, lag_count), f32),
             pltpu.VMEM(fwd.shape, BF16),
             pltpu.VMEM(band.shape, BF16),
             pltpu.VMEM(lag.shape, BF16),
+            pltpu.SemaphoreType.DMA((windows,)),
             pltpu.SemaphoreType.DMA((3,)),
             pltpu.SemaphoreType.DMA((chan_count,)),
             pltpu.SemaphoreType.DMA((chan_count,)),
             pltpu.SemaphoreType.DMA((chan_count,)),
             pltpu.SemaphoreType.DMA((chan_count,)),
-            pltpu.SemaphoreType.DMA((win_count,)),
-            pltpu.SemaphoreType.DMA((win_count,)),
-            pltpu.SemaphoreType.DMA((win_count,)),
+            pltpu.SemaphoreType.DMA((2 * win_count,)),
+            pltpu.SemaphoreType.DMA((2 * win_count,)),
+            pltpu.SemaphoreType.DMA((2 * win_count,)),
         ],
         compiler_params=pltpu.CompilerParams(
-            collective_id=0, has_side_effects=True, vmem_limit_bytes=48 * 1024 * 1024
+            collective_id=0, has_side_effects=True, vmem_limit_bytes=67_043_328
         ),
         name="interferometry",
     )(sources, records, jnp.asarray(fwd), jnp.asarray(band), jnp.asarray(lag))

time: 52.9 us -> 45.1 us (0.85)
  the two profiles are of different devices: /device:TPU:0 before, /device:TPU:6 now
where the time goes in v2:
time: 45.1 us; the launch traced here: 44.9 us
  Pallas kernels  43.2 us (96%)
  local copies, waits for them, and re-layouts  1.67 us (4%)
    pallas_call x1, Pallas kernels, fused(): pl.pallas_call(functools.partial(fused_kernel, half_width, reach, chan_co...  43.2 us
    unnamed x1, local copies, waits for them, and re-layouts  1.67 us

profile of v2, /device:TPU:6, one launch (start us, length us, event | category | flops | bytes accessed | tf_op | source)
XLA Modules:
  0.0 44.9 jit_solution(10700741588932456333)
XLA Ops:
  0.0 43.2 %interferometry.1 = f32[256,256]{1,0:T(8,128)} custom-call(s32[32]{0:T(128)} %src_ref.1, f32[4,128,256]{2,1,0:T(8,128)} %rec_hbm.1, bf16[2,4,256,256]{3,2,1,0:T(8,128)(2,1)} %constant.6.clone.fwd_hbm, bf16[512,512]{1,0:T(8,128)(2,1)} %constant.7.clone.band_hbm, bf16[2,1024,256]{2,1,0:T(8,128)(2,1)} %constant.8.clone.lag_hbm), custom_call_target="tpu_custom_call" | custom-call | tf_op jit(solution)/shard_map/interferometry/pallas_call | solution.py:473
  43.3 1.7 %copy.7 = f32[8,256,32]{1,2,0:T(8,128)} copy(f32[8,256,32]{1,2,0:T(8,128)} %bitcast.3) | data formatting | bytes 524288

commit v3 on v2

--- a/solution.py
+++ b/solution.py
@@ -113,6 +113,7 @@
 
 
 LANES = 128
+PIECES = 2
 BF16 = jnp.bfloat16
 MESH = pl.DeviceIdType.MESH
 
@@ -304,12 +305,16 @@
             at = 2 * (windows * i + w)
             gs[me, at : at + 1, :] = wr[pl.ds(w * width + owned, 1), :]
             gs[me, at + 1 : at + 2, :] = wi[pl.ds(w * width + owned, 1), :]
-    gather = {}
-    for d in (4, 5, 1, 6, 7, 2, 3):
-        gather[d] = pltpu.make_async_remote_copy(
-            src_ref=gs.at[me], dst_ref=gs.at[me], send_sem=g_send.at[d], recv_sem=g_recv.at[d],
-            device_id={"chan": flipped(d)}, device_id_type=MESH,
+    def passing(block, target):
+        slot = gs.at[flipped(block)]
+        return pltpu.make_async_remote_copy(
+            src_ref=slot, dst_ref=slot, send_sem=g_send.at[block ^ target],
+            recv_sem=g_recv.at[block ^ target], device_id={"chan": flipped(target)},
+            device_id_type=MESH,
         )
+
+    gather = {b ^ t: passing(b, t) for b, t in ((0, 4), (0, 2), (0, 1), (4, 1), (4, 2), (2, 1), (6, 1))}
+    for d in (4, 2, 1):
         gather[d].start()
     tables[2].wait()
 
@@ -347,10 +352,14 @@
                     cl[i * width : (i + 1) * width, col : col + LANES] = low
         part[device] = dot(ch[...], lag[0]) + dot(cl[...], lag[0]) + dot(ch[...], lag[1])
 
-    def hop(slot, landing, sem, target):
+    piece = part.shape[1] // PIECES
+
+    def hop(slot, k, landing, sem, target):
+        at = pl.ds(k * piece, piece)
         return pltpu.make_async_remote_copy(
-            src_ref=part.at[slot], dst_ref=landing.at[slot], send_sem=r_send.at[slot],
-            recv_sem=sem.at[slot], device_id={"win": target}, device_id_type=MESH,
+            src_ref=part.at[slot, at], dst_ref=landing.at[slot, at],
+            send_sem=r_send.at[slot * PIECES + k], recv_sem=sem.at[slot * PIECES + k],
+            device_id={"win": target}, device_id_type=MESH,
         )
 
     def finish(owner, half):
@@ -358,30 +367,47 @@
 
         @pl.when(owner > row)
         def _():
-            right = hop(slot, from_left, left_sem, row + 1)
-
-            @pl.when(row > 0)
-            def _():
-                right.wait_recv()
-                part[slot] = part[slot] + from_left[slot]
-
-            right.start()
+            for k in range(PIECES):
+                right = hop(slot, k, from_left, left_sem, row + 1)
+
+                @pl.when(row > 0)
+                def _():
+                    right.wait_recv()
+                    at = slice(k * piece, (k + 1) * piece)
+                    part[slot, at] = part[slot, at] + from_left[slot, at]
+
+                right.start()
 
         @pl.when(owner < row)
         def _():
-            left = hop(slot, from_right, right_sem, row - 1)
-
-            @pl.when(row < win_count - 1)
-            def _():
-                left.wait_recv()
-                part[slot] = part[slot] + from_right[slot]
-
-            left.start()
+            for k in range(PIECES):
+                left = hop(slot, k, from_right, right_sem, row - 1)
+
+                @pl.when(row < win_count - 1)
+                def _():
+                    left.wait_recv()
+                    at = slice(k * piece, (k + 1) * piece)
+                    part[slot, at] = part[slot, at] + from_right[slot, at]
+
+                left.start()
 
     def step(q, _):
         owner, half, d = chunk_of(q)
 
-        @pl.when(d > 0)
+        @pl.when(q == 2 * (1 - away))
+        def _():
+            gather[4].wait_recv()
+            gather[6].start()
+            gather[5].start()
+            gather[2].wait_recv()
+            gather[3].start()
+
+        @pl.when(q == 2 * (2 - away))
+        def _():
+            gather[6].wait_recv()
+            gather[7].start()
+
+        @pl.when(lax.rem(q, 2) == 1)
         def _():
             pltpu.make_async_remote_copy(
                 src_ref=gs.at[me], dst_ref=gs.at[me], send_sem=g_send.at[d], recv_sem=g_recv.at[d],
@@ -394,9 +420,9 @@
         def _():
             finish(owner, half)
 
-        @pl.when((inner == 1) & (q >= 4) & (q < 6))
-        def _():
-            first, side, _ = chunk_of(q - 4)
+        @pl.when((inner == 1) & (q >= 2) & (q < 4))
+        def _():
+            first, side, _ = chunk_of(q - 2)
             finish(first, side)
 
         return 0
@@ -432,12 +458,14 @@
 
         @pl.when(row < win_count - 1)
         def _():
-            hop(slot, from_right, right_sem, row + 1).wait_recv()
+            for j in range(PIECES):
+                hop(slot, j, from_right, right_sem, row + 1).wait_recv()
             out_ref[at, :] += from_right[slot]
 
         @pl.when(row > 0)
         def _():
-            hop(slot, from_left, left_sem, row - 1).wait_recv()
+            for j in range(PIECES):
+                hop(slot, j, from_left, left_sem, row - 1).wait_recv()
             out_ref[at, :] += from_left[slot]
 
     for copy in exchange + list(gather.values()):
@@ -445,7 +473,8 @@
     for slot in range(chunks):
         @pl.when(row != slot // 2)
         def _():
-            hop(slot, from_left, left_sem, lax.rem(row + 1, win_count)).wait_send()
+            for k in range(PIECES):
+                hop(slot, k, from_left, left_sem, lax.rem(row + 1, win_count)).wait_send()
 
 
 def fused(records, sources):
@@ -501,9 +530,9 @@
             pltpu.SemaphoreType.DMA((chan_count,)),
             pltpu.SemaphoreType.DMA((chan_count,)),
             pltpu.SemaphoreType.DMA((chan_count,)),
-            pltpu.SemaphoreType.DMA((2 * win_count,)),
-            pltpu.SemaphoreType.DMA((2 * win_count,)),
-            pltpu.SemaphoreType.DMA((2 * win_count,)),
+            pltpu.SemaphoreType.DMA((2 * win_count * PIECES,)),
+            pltpu.SemaphoreType.DMA((2 * win_count * PIECES,)),
+            pltpu.SemaphoreType.DMA((2 * win_count * PIECES,)),
         ],
         compiler_params=pltpu.CompilerParams(
             collective_id=0, has_side_effects=True, vmem_limit_bytes=67_043_328

time: 45.1 us -> 40.7 us (0.902)
  Pallas kernels: 43.2 us -> 38.8 us
    pallas_call x1, Pallas kernels: 43.2 us -> 38.8 us  [fused(): pl.pallas_call(functools.partial(fused_kernel, half_width, reach, chan_co...]
where the time goes in v3:
time: 40.7 us; the launch traced here: 40.5 us
  Pallas kernels  38.8 us (95%)
  local copies, waits for them, and re-layouts  1.67 us (4%)
    pallas_call x1, Pallas kernels, fused(): pl.pallas_call(functools.partial(fused_kernel, half_width, reach, chan_co...  38.8 us
    unnamed x1, local copies, waits for them, and re-layouts  1.67 us

profile of v3, /device:TPU:6, one launch (start us, length us, event | category | flops | bytes accessed | tf_op | source)
XLA Modules:
  0.0 40.5 jit_solution(13187922955573044232)
XLA Ops:
  0.0 38.8 %interferometry.1 = f32[256,256]{1,0:T(8,128)} custom-call(s32[32]{0:T(128)} %src_ref.1, f32[4,128,256]{2,1,0:T(8,128)} %rec_hbm.1, bf16[2,4,256,256]{3,2,1,0:T(8,128)(2,1)} %constant.6.clone.fwd_hbm, bf16[512,512]{1,0:T(8,128)(2,1)} %constant.7.clone.band_hbm, bf16[2,1024,256]{2,1,0:T(8,128)(2,1)} %constant.8.clone.lag_hbm), custom_call_target="tpu_custom_call" | custom-call | tf_op jit(solution)/shard_map/interferometry/pallas_call | solution.py:502
  38.9 1.7 %copy.7 = f32[8,256,32]{1,2,0:T(8,128)} copy(f32[8,256,32]{1,2,0:T(8,128)} %bitcast.3) | data formatting | bytes 524288

commit v4 on v3

--- a/solution.py
+++ b/solution.py
@@ -113,7 +113,7 @@
 
 
 LANES = 128
-PIECES = 2
+PIECES = 4
 BF16 = jnp.bfloat16
 MESH = pl.DeviceIdType.MESH
 
@@ -535,7 +535,7 @@
             pltpu.SemaphoreType.DMA((2 * win_count * PIECES,)),
         ],
         compiler_params=pltpu.CompilerParams(
-            collective_id=0, has_side_effects=True, vmem_limit_bytes=67_043_328
+            collective_id=0, has_side_effects=True, vmem_limit_bytes=66_400_000
         ),
         name="interferometry",
     )(sources, records, jnp.asarray(fwd), jnp.asarray(band), jnp.asarray(lag))

time: 40.7 us -> 40.6 us (level)
  no operation moved by 1% of the time
where the time goes in v4:
time: 40.6 us; the launch traced here: 40.4 us
  Pallas kernels  38.7 us (95%)
  local copies, waits for them, and re-layouts  1.67 us (4%)
    pallas_call x1, Pallas kernels, fused(): pl.pallas_call(functools.partial(fused_kernel, half_width, reach, chan_co...  38.7 us
    unnamed x1, local copies, waits for them, and re-layouts  1.67 us

profile of v4, /device:TPU:6, one launch (start us, length us, event | category | flops | bytes accessed | tf_op | source)
XLA Modules:
  0.0 40.4 jit_solution(11144432572438474237)
XLA Ops:
  0.0 38.7 %interferometry.1 = f32[256,256]{1,0:T(8,128)} custom-call(s32[32]{0:T(128)} %src_ref.1, f32[4,128,256]{2,1,0:T(8,128)} %rec_hbm.1, bf16[2,4,256,256]{3,2,1,0:T(8,128)(2,1)} %constant.6.clone.fwd_hbm, bf16[512,512]{1,0:T(8,128)(2,1)} %constant.7.clone.band_hbm, bf16[2,1024,256]{2,1,0:T(8,128)(2,1)} %constant.8.clone.lag_hbm), custom_call_target="tpu_custom_call" | custom-call | tf_op jit(solution)/shard_map/interferometry/pallas_call | solution.py:502
  38.7 1.7 %copy.7 = f32[8,256,32]{1,2,0:T(8,128)} copy(f32[8,256,32]{1,2,0:T(8,128)} %bitcast.3) | data formatting | bytes 524288
